TPU v7x, 512 devices: a whole 4x4x16 slice. The times are simulated.
512 devices in a mesh: dp: 64 (over z_lo, x, core), tensor: 8 (over y, z_hi).
Axes of the slice: x: 4, y: 4, z: 16 (z_hi: 2, z_lo: 8; z = z_hi * 8 + z_lo), core: 2. Of those that a mesh axis runs over, the one named last changes fastest.
Arguments:
- o_inputs: bfloat16 [16384, 8192], P('dp', 'tensor'), may hold values from -6 to 6
- o_gradients: bfloat16 [16384, 8192], P('dp', 'tensor'), may hold values from -6 to 6
- up_inputs: bfloat16 [16384, 8192], P('dp', 'tensor'), may hold values from -6 to 6
- up_gradients: bfloat16 [16384, 28672], P('dp', 'tensor'), may hold values from -6 to 6
- o_in_proj: bfloat16 [8192, 32], P('tensor'), may hold values from -0.0625 to 0.0625
- o_out_proj: bfloat16 [8192, 32], P('tensor'), may hold values from -0.0625 to 0.0625
- up_in_proj: bfloat16 [8192, 32], P('tensor'), may hold values from -0.0625 to 0.0625
- up_out_proj: bfloat16 [28672, 32], P('tensor'), may hold values from -0.03125 to 0.03125
- segment_ids: int32 [64, 256], P('dp'), may hold values from 0 to 3, never falling along the last dimension, each value on 1 to 128 neighbouring positions
- owner_map: int32 [64], replicated, may hold values from 0 to 63, each once
Outputs:
- example_vectors: float32 [2, 256, 1024], P(None, 'dp', 'tensor')
- fisher_owned: float32 [64, 32, 1024], P('dp', None, 'tensor')
Inputs may be any that keep to these rules, and one draw needn't show every extreme that they name: `segment_ids`: within each row, ids never fall; each of the 4 ids holds 1 to 128 tokens, and one holds exactly that many. `owner_map`: each block index appears exactly once.
All inputs are finite; a program needn't handle non-finite values.
Results may differ from a plain program's by a relative error of at most 0.0003.
Values sent between devices are 32-bit elements; how exact they have to be, the bound alone decides.
A program may use at most 64 MiB of HBM per device.

v0:
```python
import jax
import jax.numpy as jnp
from jax import lax
from jax.sharding import PartitionSpec as P

TOK_DEV = 256
EX_DEV = 4


def local_vectors(segments, in_o, out_o, in_up, out_up):
    examples_local = EX_DEV
    onehot = (segments[:, None] == jnp.arange(examples_local, dtype=jnp.int32)[None, :]).astype(
        jnp.float32
    )
    vector_scale = (EX_DEV / TOK_DEV) ** 0.5
    results = []
    for in_low, out_low in ((in_o, out_o), (in_up, out_up)):
        outers = (out_low[:, :, None] * in_low[:, None, :]).reshape(in_low.shape[0], -1)
        summed = jnp.dot(onehot.T, outers, precision=lax.Precision.HIGHEST)
        results.append(summed * vector_scale)
    return jnp.concatenate(results, axis=1)


def shards(
    o_inputs,
    o_gradients,
    up_inputs,
    up_gradients,
    o_in_proj,
    o_out_proj,
    up_in_proj,
    up_out_proj,
    segment_ids,
    owner_map,
):
    tensor_index = lax.axis_index("tensor")
    tensor_count = lax.axis_size("tensor")
    dp_count = lax.axis_size("dp")
    width = o_in_proj.shape[1] * o_out_proj.shape[1]
    col_width = width // tensor_count
    own_rows = 2 * width // dp_count
    examples_total = EX_DEV * dp_count
    segments = segment_ids[0]
    partials = (
        jnp.dot(o_inputs, o_in_proj, preferred_element_type=jnp.float32),
        jnp.dot(o_gradients, o_out_proj, preferred_element_type=jnp.float32),
        jnp.dot(up_inputs, up_in_proj, preferred_element_type=jnp.float32),
        jnp.dot(up_gradients, up_out_proj, preferred_element_type=jnp.float32),
    )
    in_o, out_o, in_up, out_up = lax.psum(
        (partials[0], partials[1], partials[2], partials[3]), "tensor"
    )
    stacked_vectors = local_vectors(segments, in_o, out_o, in_up, out_up)
    examples_local = stacked_vectors.shape[0]
    by_projection = stacked_vectors.reshape(examples_local, 2, width).transpose(1, 0, 2)
    example_vectors = lax.dynamic_slice_in_dim(
        by_projection, tensor_index * col_width, col_width, 2
    )
    block_range = jnp.arange(owner_map.shape[0], dtype=jnp.int32)

    def block_product(source, owner_block):
        row_part = lax.dynamic_slice_in_dim(source, owner_block * own_rows, own_rows, 1)
        projection = owner_block * own_rows // width
        col_part = lax.dynamic_slice_in_dim(
            source, projection * width + tensor_index * col_width, col_width, 1
        )
        return jnp.dot(row_part.T, col_part, precision=lax.Precision.HIGHEST)

    block_count = lax.axis_size("dp") * own_rows // own_rows
    block_ids = jnp.arange(block_count, dtype=jnp.int32)
    matches = block_ids[:, None] == block_range[None, :]
    owners = jnp.sum(jnp.where(matches, owner_map[None, :], 0), axis=1)
    blocks_done = jax.vmap(lambda owner_block: block_product(stacked_vectors, owner_block))(owners)
    fisher_block = lax.psum_scatter(
        blocks_done.reshape(lax.axis_size("dp") * own_rows, col_width) / examples_total,
        "dp",
        scatter_dimension=0,
        tiled=True,
    )
    return (example_vectors, fisher_block[None])


def solution(mesh):
    in_specs = (
        P("dp", "tensor"),
        P("dp", "tensor"),
        P("dp", "tensor"),
        P("dp", "tensor"),
        P("tensor", None),
        P("tensor", None),
        P("tensor", None),
        P("tensor", None),
        P("dp", None),
        P(),
    )
    out_specs = (P(None, "dp", "tensor"), P("dp", None, "tensor"))
    return jax.shard_map(shards, mesh=mesh, in_specs=in_specs, out_specs=out_specs, check_vma=False)
```

profile of v0, /device:TPU:1, one launch (start us, length us, event | category | flops | bytes accessed | tf_op | source)
XLA Modules:
  0.0 775.6 jit_solution(13834082860547253541)
XLA Ops:
  7.2 2.1 fusion.5
  9.3 1.9 fusion.6
  11.3 2.2 fusion.7
  13.4 0.9 fusion.8
  14.6 151.6 %all-reduce.5.cloned.1.call-done = (f32[256,32]{0,1:T(8,128)}, f32[256,32]{0,1:T(8,128)}, f32[256,32]{0,1:T(8,128)}, f32[256,32]{0,1:T(8,128)}) async-done(((f32[256,32]{0,1:T(8,128)}, f32[256,32]{0,1:T(8,128)}, f32[256,32]{0,1:T(8,128)}, f32[256,32]{0,1:T(8,128)}), (f32[256,32]{0,1:T(8,128)}, f32[256,32]{0,1:T(8,128)}, f32[256,32]{0,1:T(8,128)}, f32[256,32]{0,1:T(8,128)})) %all-reduce.5.cloned.1.call-update) | async-done | bytes 131088 | tf_op jit(solution)/shard_map/psum | solution.py:50
  166.2 1.1 broadcast_multiply_fusion
  168.5 90.9 %while.3 = (s32[]{:T(128)}, f32[4,2048]{1,0:T(4,128)S(1)}, s32[64,2]{0,1:T(2,128)S(1)}, f32[64,4,128]{2,1,0:T(4,128)S(1)}, s32[]{:T(128)}) while((s32[]{:T(128)}, f32[4,2048]{1,0:T(4,128)S(1)}, s32[64,2]{0,1:T(2,128)S(1)}, f32[64,4,128]{2,1,0:T(4,128)S(1)}, s32[]{:T(128)}) %tuple.36), condition=%wide.while_cond.1, body=%wide.while_body.1.sunk | while | flops 2 | bytes 4193 | solution.py:64
  169.2 0.8 bitcast_dynamic-update-slice_fusion.5
  170.6 0.8 bitcast_dynamic-update-slice_fusion.5
  172.1 0.8 bitcast_dynamic-update-slice_fusion.5
  173.5 0.8 bitcast_dynamic-update-slice_fusion.5
  174.9 0.8 bitcast_dynamic-update-slice_fusion.5
  176.3 0.8 bitcast_dynamic-update-slice_fusion.5
  177.7 0.8 bitcast_dynamic-update-slice_fusion.5
  179.1 0.8 bitcast_dynamic-update-slice_fusion.5
  180.6 0.8 bitcast_dynamic-update-slice_fusion.5
  182.0 0.8 bitcast_dynamic-update-slice_fusion.5
  183.4 0.8 bitcast_dynamic-update-slice_fusion.5
  184.8 0.8 bitcast_dynamic-update-slice_fusion.5
  187.7 0.8 bitcast_dynamic-update-slice_fusion.5
  189.1 0.8 bitcast_dynamic-update-slice_fusion.5
  190.5 0.8 bitcast_dynamic-update-slice_fusion.5
  191.9 0.8 bitcast_dynamic-update-slice_fusion.5
  193.3 0.8 bitcast_dynamic-update-slice_fusion.5
  194.8 0.8 bitcast_dynamic-update-slice_fusion.5
  196.2 0.8 bitcast_dynamic-update-slice_fusion.5
  197.6 0.8 bitcast_dynamic-update-slice_fusion.5
  199.0 0.8 bitcast_dynamic-update-slice_fusion.5
  200.4 0.8 bitcast_dynamic-update-slice_fusion.5
  259.4 84.2 %while.2 = (s32[]{:T(128)}, f32[4,2048]{1,0:T(4,128)S(1)}, s32[64,2]{0,1:T(2,128)S(1)}, f32[64,4,32]{2,1,0:T(4,128)S(1)}, s32[]{:T(128)}) while((s32[]{:T(128)}, f32[4,2048]{1,0:T(4,128)S(1)}, s32[64,2]{0,1:T(2,128)S(1)}, f32[64,4,32]{2,1,0:T(4,128)S(1)}, s32[]{:T(128)}) %tuple.44), condition=%wide.while_cond, body=%wide.while_body.sunk | while | flops 2 | bytes 4193 | solution.py:62
  343.6 2.8 convolution_multiply_fusion
  347.0 421.7 %reduce-scatter.2.cloned.1.call-done = f32[32,128]{1,0:T(8,128)} async-done(((f32[2048,128]{1,0:T(8,128)}), f32[32,128]{1,0:T(8,128)}) %reduce-scatter.2.cloned.1.call-update) | async-done | bytes 16400 | tf_op jit(solution)/shard_map/reduce_scatter | solution.py:74
  (386 shorter events, 160.2 us)
Async XLA Ops:
  7.2 4.1 copy-start
  7.2 6.3 copy-start.1
  7.2 6.3 copy-start.2
  7.2 159.0 %all-reduce.5.cloned.1.call-start = ((), (), s32[]{:S(2)}) async-start(), calls=%async_computation.2 | async-start | bytes 262144 | tf_op jit(solution)/shard_map/psum | solution.py:50
  9.3 5.1 copy-start.4
  13.4 153.8 %copy-start.3 = (s32[1,256]{1,0:T(1,128)S(1)}, s32[1,256]{1,0:T(1,128)}, u32[]{:S(2)}) copy-start(s32[1,256]{1,0:T(1,128)} %param.18) | copy-start | bytes 3076
  14.3 754.4 %reduce-scatter.2.cloned.1.call-start = ((), (), s32[]{:S(2)}) async-start(), calls=%async_computation.1 | async-start | bytes 1064960 | tf_op jit(solution)/shard_map/reduce_scatter | solution.py:74
Sparse Core Ops, SparseCore 0:
  14.5 151.7 all-reduce.4
  346.6 422.1 reduce-scatter.1
where the time goes:
time: 786 us; the launch traced here: 776 us
  waiting for transfers between devices  573 us (73%)
  local copies, waits for them, and re-layouts  176 us (22%)
  between operations  14.1 us (2%)
  matrix products  11.1 us (1%)
    reduce_scatter x1, waiting for transfers between devices, shards(): lax.psum_scatter(blocks_done.reshape(lax.axis_size('dp') * own_rows, col_...  422 us
    gather x384, local copies, waits for them, and re-layouts  175 us
    psum x1, waiting for transfers between devices, shards(): lax.psum((partials[0], partials[1], partials[2], partials[3]), 'tensor')  152 us
  transfers between devices with their start and end apart: 2, of which 2 were waited for; matrix products, arithmetic and copies ran while one was open for 0% of the time, Pallas kernels for 0%

commit v1 on v0

v1 whole, which is shorter than its diff:
```python
import functools

import jax
import jax.numpy as jnp
from jax import lax
from jax.experimental import pallas as pl
from jax.experimental.pallas import tpu as pltpu
from jax.sharding import PartitionSpec as P

TOK = 256
EX = 4
KP = 32
BLOCKS = 64
EXAMPLES = 256
YN = 4
HIGH = lax.Precision.HIGHEST
MESH = pl.DeviceIdType.MESH
NT = (((1,), (1,)), ((), ()))
TN = (((0,), (0,)), ((), ()))


def kernel(
    n_dp,
    xo_ref, go_ref, xu_ref, gu_ref, pxo_ref, pgo_ref, pxu_ref, pgu_ref, seg_ref, own_ref,
    ev_ref, f_ref,
    xo, go, xu, gu, pxo, pgo, pxu, pgu, seg_v, own_v, ev, f_v,
    part, recv_y, recv_z, sum_z, full, g_ref, v_ref, send_d, recv_d,
    in_sem, out_sem, sy_sem, ry_sem, sz_sem, rz_sem, sg_sem, rg_sem, sd_sem, rd_sem,
):
    d = lax.axis_index("dp")
    t = lax.axis_index("tensor")
    y, zh = t // 2, lax.rem(t, 2)
    partner = y * 2 + (1 - zh)

    def y_peer(j):
        return lax.rem(y + j, YN)

    half = TOK // 2
    loads = [
        (pxo_ref, pxo), (xo_ref, xo), (pgo_ref, pgo), (go_ref, go), (pxu_ref, pxu), (xu_ref, xu), (pgu_ref, pgu),
        (gu_ref.at[pl.ds(0, half)], gu.at[pl.ds(0, half)]), (gu_ref.at[pl.ds(half, half)], gu.at[pl.ds(half, half)]),
        (seg_ref, seg_v), (own_ref, own_v),
    ]
    copies = [pltpu.make_async_copy(s, dst, in_sem.at[i]) for i, (s, dst) in enumerate(loads)]
    for c in copies:
        c.start()

    barrier = pltpu.get_barrier_semaphore()
    for j in range(1, YN):
        pl.semaphore_signal(barrier, inc=1, device_id={"tensor": y_peer(j) * 2 + zh}, device_id_type=MESH)
    pl.semaphore_signal(barrier, inc=1, device_id={"tensor": partner}, device_id_type=MESH)

    def greet(k, carry):
        pl.semaphore_signal(barrier, inc=1, device_id={"dp": lax.rem(d + k, n_dp)}, device_id_type=MESH)
        return carry

    lax.fori_loop(1, n_dp, greet, 0)

    def project(w, x):
        return lax.dot_general(w, x, NT, preferred_element_type=jnp.float32)

    def y_send(i):
        return pltpu.make_async_remote_copy(
            src_ref=part.at[i], dst_ref=recv_y.at[y], send_sem=sy_sem.at[i], recv_sem=ry_sem.at[y],
            device_id={"tensor": i * 2 + zh}, device_id_type=MESH,
        )

    for i, (w, x) in enumerate(((pxo, xo), (pgo, go), (pxu, xu), (pgu, gu))):
        copies[2 * i].wait()
        copies[2 * i + 1].wait()
        if i < 3:
            part[i] = project(w[...], x[...])
        else:
            part[i, :, pl.ds(0, half)] = project(w[...], x[pl.ds(0, half), :])
            copies[8].wait()
            part[i, :, pl.ds(half, half)] = project(w[...], x[pl.ds(half, half), :])
        if i == 0:
            pl.semaphore_wait(barrier, YN + n_dp - 1)

        @pl.when(y != i)
        def _():
            y_send(i).start()

    total = part[y]
    for j in range(1, YN):
        p = y_peer(j)
        pltpu.make_async_remote_copy(
            src_ref=part.at[p], dst_ref=recv_y.at[p], send_sem=sy_sem.at[p], recv_sem=ry_sem.at[p],
            device_id={"tensor": p * 2 + zh}, device_id_type=MESH,
        ).wait_recv()
        total += recv_y[p]
    sum_z[...] = total
    zcopy = pltpu.make_async_remote_copy(
        src_ref=sum_z, dst_ref=recv_z, send_sem=sz_sem, recv_sem=rz_sem,
        device_id={"tensor": partner}, device_id_type=MESH,
    )
    zcopy.start()
    zcopy.wait_recv()
    full[y] = total + recv_z[...]
    gathers = []
    for j in range(1, YN):
        p = y_peer(j)
        c = pltpu.make_async_remote_copy(
            src_ref=full.at[y], dst_ref=full.at[y], send_sem=sg_sem.at[j - 1], recv_sem=rg_sem.at[y],
            device_id={"tensor": p * 2 + zh}, device_id_type=MESH,
        )
        c.start()
        gathers.append(c)
    for j in range(1, YN):
        p = y_peer(j)
        pltpu.make_async_remote_copy(
            src_ref=full.at[p], dst_ref=full.at[p], send_sem=sg_sem.at[j - 1], recv_sem=rg_sem.at[p],
            device_id={"tensor": p * 2 + zh}, device_id_type=MESH,
        ).wait_recv()

    copies[9].wait()
    copies[10].wait()
    seg = seg_v[...]
    scale = (EX / TOK) ** 0.5
    masks = [jnp.where(seg == e, scale, 0.0).astype(jnp.float32) for e in range(EX)]
    group = lax.broadcasted_iota(jnp.int32, (EX * KP // 4, 128), 1) // KP
    by_block = []
    for p in range(2):
        low, high = full[2 * p], full[2 * p + 1]
        high_e = jnp.concatenate([high * m for m in masks], axis=0)
        low_e = jnp.concatenate([low * m for m in masks], axis=0)
        low_4 = jnp.concatenate([low] * 4, axis=0)
        g_ref[...] = lax.dot_general(high_e, low_4, NT, precision=HIGH, preferred_element_type=jnp.float32)
        rows = [g_ref[pl.ds(j, EX * KP // 4, stride=4), :] for j in range(4)]
        v_ref[p] = jnp.where(group == 0, rows[0], jnp.where(group == 1, rows[1], jnp.where(group == 2, rows[2], rows[3])))
        by_block.append(lax.dot_general(high, low_e, NT, precision=HIGH, preferred_element_type=jnp.float32))
        ev[p] = v_ref[p, pl.ds(t, EX, stride=8), :]
    ev_out = pltpu.make_async_copy(ev, ev_ref, out_sem.at[0])
    ev_out.start()

    table = jnp.concatenate(
        [jnp.concatenate(by_block, axis=0), (lax.broadcasted_iota(jnp.int32, (BLOCKS, 128), 0) >= KP).astype(jnp.float32)], axis=1
    )
    onehot = (lax.broadcasted_iota(jnp.int32, (BLOCKS, n_dp), 0) == own_v[...]).astype(jnp.float32)
    picked = lax.dot_general(onehot, table, TN, precision=HIGH, preferred_element_type=jnp.float32)
    is_up = picked[:, 128:] > 0.5
    for e in range(EX):
        o_row = jnp.broadcast_to(v_ref[0, pl.ds(t + 8 * e, 1), :], (n_dp, 128))
        up_row = jnp.broadcast_to(v_ref[1, pl.ds(t + 8 * e, 1), :], (n_dp, 128))
        send_d[:, e, :] = jnp.where(is_up, up_row, o_row)
    send_d[:, EX, :] = picked[:, :128]

    def d_copy(dst):
        return pltpu.make_async_remote_copy(
            src_ref=send_d.at[dst, pl.ds(0, EX + 1)], dst_ref=recv_d.at[d, pl.ds(0, EX + 1)],
            send_sem=sd_sem, recv_sem=rd_sem, device_id={"dp": dst}, device_id_type=MESH,
        )

    def d_send(k, carry):
        d_copy(lax.rem(d + k, n_dp)).start()
        return carry

    lax.fori_loop(1, n_dp, d_send, 0)
    recv_d[d] = send_d[d]
    whole = pltpu.make_async_remote_copy(
        src_ref=send_d.at[pl.ds(0, n_dp - 1), pl.ds(0, EX + 1)], dst_ref=recv_d.at[pl.ds(0, n_dp - 1), pl.ds(0, EX + 1)],
        send_sem=sd_sem, recv_sem=rd_sem, device_id={"dp": lax.rem(d + 1, n_dp)}, device_id_type=MESH,
    )
    whole.wait_recv()
    rows_t = recv_d[:, EX, :].T
    fisher = jnp.zeros((KP, 128), jnp.float32)
    for e in range(EX):
        fisher += jnp.dot(
            rows_t[e * KP:(e + 1) * KP], recv_d[:, e, :], precision=HIGH, preferred_element_type=jnp.float32
        )
    f_v[0] = fisher * (1.0 / EXAMPLES)
    f_out = pltpu.make_async_copy(f_v, f_ref, out_sem.at[1])
    f_out.start()

    for i in range(YN):
        @pl.when(y != i)
        def _():
            y_send(i).wait_send()
    zcopy.wait_send()
    for c in gathers:
        c.wait_send()
    whole.wait_send()
    ev_out.wait()
    f_out.wait()


def shards(xo, go, xu, gu, pxo, pgo, pxu, pgu, seg, owner):
    n_dp = lax.axis_size("dp")
    k1, k2 = xo.shape[1], gu.shape[1]
    bf, f32 = jnp.bfloat16, jnp.float32
    hbm = pl.BlockSpec(memory_space=pltpu.HBM)
    dma = pltpu.SemaphoreType.DMA
    return pl.pallas_call(
        functools.partial(kernel, n_dp),
        out_shape=(jax.ShapeDtypeStruct((2, EX, 128), f32), jax.ShapeDtypeStruct((1, KP, 128), f32)),
        in_specs=[hbm] * 10,
        out_specs=(hbm, hbm),
        scratch_shapes=[
            pltpu.VMEM((TOK, k1), bf), pltpu.VMEM((TOK, k1), bf), pltpu.VMEM((TOK, k1), bf), pltpu.VMEM((TOK, k2), bf),
            pltpu.VMEM((KP, k1), bf), pltpu.VMEM((KP, k1), bf), pltpu.VMEM((KP, k1), bf), pltpu.VMEM((KP, k2), bf),
            pltpu.VMEM((1, TOK), jnp.int32), pltpu.VMEM((1, owner.shape[0]), jnp.int32),
            pltpu.VMEM((2, EX, 128), f32), pltpu.VMEM((1, KP, 128), f32),
            pltpu.VMEM((4, KP, TOK), f32), pltpu.VMEM((YN, KP, TOK), f32), pltpu.VMEM((KP, TOK), f32),
            pltpu.VMEM((KP, TOK), f32), pltpu.VMEM((4, KP, TOK), f32), pltpu.VMEM((128, 128), f32), pltpu.VMEM((2, KP, 128), f32),
            pltpu.VMEM((n_dp, 8, 128), f32), pltpu.VMEM((n_dp, 8, 128), f32),
            dma((11,)), dma((2,)), dma((4,)), dma((4,)), dma, dma, dma((3,)), dma((4,)), dma, dma,
        ],
        compiler_params=pltpu.CompilerParams(collective_id=0, has_side_effects=True, vmem_limit_bytes=60 << 20),
    )(xo, go, xu, gu, pxo.T, pgo.T, pxu.T, pgu.T, seg, owner.reshape(1, -1))


def solution(mesh):
    in_specs = (P("dp", "tensor"),) * 4 + (P("tensor", None),) * 4 + (P("dp", None), P())
    out_specs = (P(None, "dp", "tensor"), P("dp", None, "tensor"))
    return jax.shard_map(shards, mesh=mesh, in_specs=in_specs, out_specs=out_specs, check_vma=False)
```

time: 786 us -> 47.9 us (0.06); the launches traced: 776 us -> 47.7 us
  waiting for transfers between devices: 573 us -> 0 us
  local copies, waits for them, and re-layouts: 176 us -> 2.59 us
  Pallas kernels: 0 us -> 44.4 us
  between operations: 14.1 us -> 0.64 us
  matrix products: 11.1 us -> 0 us
    reduce_scatter x1 -> x0, waiting for transfers between devices: 422 us -> none  [shards(): lax.psum_scatter(blocks_done.reshape(lax.axis_size('dp') * own_rows, col_...]
    gather x384 -> x0, local copies, waits for them, and re-layouts: 175 us -> none
    psum x1 -> x0, waiting for transfers between devices: 152 us -> none  [shards(): lax.psum((partials[0], partials[1], partials[2], partials[3]), 'tensor')]
    pallas_call x0 -> x1, Pallas kernels: none -> 44.4 us  [shards(): pl.pallas_call(functools.partial(kernel, n_dp), out_shape=(jax.ShapeDtype...]
    dot_general x7 -> x0, matrix products: 11.1 us -> none  [the longest x1 2.8 us: block_product(): return jnp.dot(row_part.T, col_part, precision=lax.Precision.HIGHEST)]
  transfers between devices with their start and end apart: 2 -> 0, of which waited for: 2 -> 0; matrix products, arithmetic and copies ran while one was open for 0% -> 0% of each run, Pallas kernels for 0% -> 0%
where the time goes in v1:
time: 47.9 us; the launch traced here: 47.7 us
  Pallas kernels  44.4 us (93%)
  local copies, waits for them, and re-layouts  2.59 us (5%)
  between operations  0.64 us (1%)
    pallas_call x1, Pallas kernels, shards(): pl.pallas_call(functools.partial(kernel, n_dp), out_shape=(jax.ShapeDtype...  44.4 us
    unnamed x2, local copies, waits for them, and re-layouts  2.59 us

profile of v1, /device:TPU:1, one launch (start us, length us, event | category | flops | bytes accessed | tf_op | source)
XLA Modules:
  0.0 47.7 jit_solution(16957742228308675567)
XLA Ops:
  0.6 44.4 %shard_map.113 = (f32[2,4,128]{2,1,0:T(4,128)}, f32[1,32,128]{2,1,0:T(8,128)}) custom-call(bf16[256,1024]{1,0:T(8,128)(2,1)} %xo_ref.1, bf16[256,1024]{1,0:T(8,128)(2,1)} %go_ref.1, bf16[256,1024]{1,0:T(8,128)(2,1)} %xu_ref.1, bf16[256,3584]{1,0:T(8,128)(2,1)} %gu_ref.1, bf16[32,1024]{1,0:T(8,128)(2,1)} %bitcast.6, bf16[32,1024]{1,0:T(8,128)(2,1)} %bitcast.7, ...), custom_call_target="tpu_custom_call" | custom-call | tf_op jit(solution)/shard_map/pallas_call | solution.py:193
  45.1 1.3 %copy.14 = f32[2,4,128]{2,1,0:T(4,128)} copy(f32[2,4,128]{2,1,0:T(4,128)} %get-tuple-element.4) | data formatting | bytes 8192
  46.3 1.3 %copy.15 = f32[1,32,128]{2,1,0:T(8,128)} copy(f32[1,32,128]{2,1,0:T(8,128)} %get-tuple-element.5) | data formatting | bytes 32768

commit v2 on v1

v2 whole, which is shorter than its diff:
```python
import functools

import jax
import jax.numpy as jnp
from jax import lax
from jax.experimental import pallas as pl
from jax.experimental.pallas import tpu as pltpu
from jax.sharding import PartitionSpec as P

TOK = 256
EX = 4
KP = 32
BLOCKS = 64
EXAMPLES = 256
YN = 4
PLANE = 8
HIGH = lax.Precision.HIGHEST
MESH = pl.DeviceIdType.MESH
NT = (((1,), (1,)), ((), ()))
TN = (((0,), (0,)), ((), ()))


def kernel(
    n_dp,
    xo_ref, go_ref, xu_ref, gu_ref, pxo_ref, pgo_ref, pxu_ref, pgu_ref, seg_ref, own_ref,
    ev_ref, f_ref,
    xo, go, xu, gu, pxo, pgo, pxu, pgu, seg_v, own_v, ev_s, ev_r, f_v,
    part, recv_y, seg_r, sum_z, recv_z, full, g_ref, v_ref, send_d, recv_d,
    in_sem, out_sem, sy_sem, ry_sem, seg_sem, sz_sem, rz_sem, sg_sem, rg_sem, ev_sem, sd_sem, rd_sem,
):
    d = lax.axis_index("dp")
    t = lax.axis_index("tensor")
    y, zh = t // 2, lax.rem(t, 2)
    plane = d // PLANE
    at, core = lax.rem(d, PLANE), lax.rem(d, 2)
    runs = n_dp // PLANE
    ring = 2 * runs
    mid = runs // 2
    z = zh * runs + plane
    held = lax.rem(z + mid, runs) * PLANE + at

    def on_ring(pos):
        pos = lax.rem(pos + ring, ring)
        return pos // runs, lax.rem(pos, runs)

    def ring_peer(step):
        half, line = on_ring(z + step)
        return {"dp": line * PLANE + at, "tensor": y * 2 + half}

    def y_peer(j):
        return lax.rem(y + j, YN)

    def reach(of_core, r):
        low = mid - 1 + of_core
        return lax.rem(r + low, runs) - low

    half = TOK // 2
    loads = [
        (pxo_ref, pxo), (xo_ref, xo), (pgo_ref, pgo), (go_ref, go), (pxu_ref, pxu), (xu_ref, xu), (pgu_ref, pgu),
        (gu_ref.at[pl.ds(0, half)], gu.at[pl.ds(0, half)]), (gu_ref.at[pl.ds(half, half)], gu.at[pl.ds(half, half)]),
        (seg_ref, seg_v), (own_ref, own_v),
    ]
    copies = [pltpu.make_async_copy(s, dst, in_sem.at[i]) for i, (s, dst) in enumerate(loads)]
    for c in copies:
        c.start()

    barrier = pltpu.get_barrier_semaphore()

    def greet(k, carry):
        who = lax.rem(at + k, PLANE)
        half_, line = on_ring(z - reach(lax.rem(who, 2), k // PLANE))
        pl.semaphore_signal(barrier, inc=1, device_id={"dp": line * PLANE + who, "tensor": y * 2 + half_}, device_id_type=MESH)
        return carry

    lax.fori_loop(1, n_dp, greet, 0)
    for step in (mid, -mid):
        pl.semaphore_signal(barrier, inc=1, device_id=ring_peer(step), device_id_type=MESH)
    for j in range(1, YN):
        pl.semaphore_signal(barrier, inc=1, device_id={"tensor": y_peer(j) * 2 + zh}, device_id_type=MESH)

    def project(w, x):
        return lax.dot_general(w, x, NT, preferred_element_type=jnp.float32)

    def y_send(i):
        return pltpu.make_async_remote_copy(
            src_ref=part.at[i], dst_ref=recv_y.at[y], send_sem=sy_sem.at[i], recv_sem=ry_sem.at[y],
            device_id={"tensor": i * 2 + zh}, device_id_type=MESH,
        )

    def y_start(i):
        @pl.when(y != i)
        def _():
            y_send(i).start()

    for i, (w, x) in enumerate(((pxo, xo), (pgo, go), (pxu, xu), (pgu, gu))):
        copies[2 * i].wait()
        copies[2 * i + 1].wait()
        if i < 3:
            part[i] = project(w[...], x[...])
        else:
            part[i, :, pl.ds(0, half)] = project(w[...], x[pl.ds(0, half), :])
            copies[8].wait()
            part[i, :, pl.ds(half, half)] = project(w[...], x[pl.ds(half, half), :])
        if i == 2:
            pl.semaphore_wait(barrier, n_dp - 1 + 2 + YN - 1)
            for k in range(3):
                y_start(k)
    y_start(3)
    copies[9].wait()
    copies[10].wait()
    seg_copy = pltpu.make_async_remote_copy(
        src_ref=seg_v, dst_ref=seg_r, send_sem=seg_sem.at[0], recv_sem=seg_sem.at[1], device_id=ring_peer(mid), device_id_type=MESH,
    )
    seg_copy.start()

    total = part[y]
    for j in range(1, YN):
        p = y_peer(j)
        pltpu.make_async_remote_copy(
            src_ref=part.at[p], dst_ref=recv_y.at[p], send_sem=sy_sem.at[p], recv_sem=ry_sem.at[p],
            device_id={"tensor": p * 2 + zh}, device_id_type=MESH,
        ).wait_recv()
        total += recv_y[p]
    sum_z[...] = total
    swaps = [
        pltpu.make_async_remote_copy(
            src_ref=sum_z, dst_ref=recv_z.at[i], send_sem=sz_sem.at[i], recv_sem=rz_sem.at[i],
            device_id=ring_peer(step), device_id_type=MESH,
        )
        for i, step in enumerate((mid, -mid))
    ]
    for c in swaps:
        c.start()
    for c in swaps:
        c.wait_recv()
    full[y] = recv_z[0] + recv_z[1]
    gathers = []
    for j in range(1, YN):
        p = y_peer(j)
        c = pltpu.make_async_remote_copy(
            src_ref=full.at[y], dst_ref=full.at[y], send_sem=sg_sem.at[j - 1], recv_sem=rg_sem.at[y],
            device_id={"tensor": p * 2 + zh}, device_id_type=MESH,
        )
        c.start()
        gathers.append(c)
    seg_copy.wait_recv()
    seg = seg_r[...]
    scale = (EX / TOK) ** 0.5
    masks = [jnp.where(seg == e, scale, 0.0).astype(jnp.float32) for e in range(EX)]
    onehot = (lax.broadcasted_iota(jnp.int32, (BLOCKS, n_dp), 0) == own_v[...]).astype(jnp.float32)
    for j in range(1, YN):
        p = y_peer(j)
        pltpu.make_async_remote_copy(
            src_ref=full.at[p], dst_ref=full.at[p], send_sem=sg_sem.at[j - 1], recv_sem=rg_sem.at[p],
            device_id={"tensor": p * 2 + zh}, device_id_type=MESH,
        ).wait_recv()

    group = lax.broadcasted_iota(jnp.int32, (EX * KP // 4, 128), 1) // KP
    by_block = []
    for p in range(2):
        low, high = full[2 * p], full[2 * p + 1]
        high_e = jnp.concatenate([high * m for m in masks], axis=0)
        low_e = jnp.concatenate([low * m for m in masks], axis=0)
        low_4 = jnp.concatenate([low] * 4, axis=0)
        g_ref[...] = lax.dot_general(high_e, low_4, NT, precision=HIGH, preferred_element_type=jnp.float32)
        rows = [g_ref[pl.ds(j, EX * KP // 4, stride=4), :] for j in range(4)]
        v_ref[p] = jnp.where(group == 0, rows[0], jnp.where(group == 1, rows[1], jnp.where(group == 2, rows[2], rows[3])))
        by_block.append(lax.dot_general(high, low_e, NT, precision=HIGH, preferred_element_type=jnp.float32))

    table = jnp.concatenate(
        [jnp.concatenate(by_block, axis=0), (lax.broadcasted_iota(jnp.int32, (BLOCKS, 128), 0) >= KP).astype(jnp.float32)], axis=1
    )
    picked = lax.dot_general(onehot, table, TN, precision=HIGH, preferred_element_type=jnp.float32)
    is_up = picked[:, 128:] > 0.5
    low = mid - 1 + core
    line = lax.broadcasted_iota(jnp.int32, (n_dp, 128), 0) // PLANE
    pos = z + lax.rem(line - z + low + ring, runs) - low
    far_half = lax.rem(pos + ring, ring) >= runs
    for e in range(EX):
        r = [[jnp.broadcast_to(v_ref[p, pl.ds(2 * y + h + 8 * e, 1), :], (n_dp, 128)) for h in range(2)] for p in range(2)]
        send_d[:, e, :] = jnp.where(is_up, jnp.where(far_half, r[1][1], r[1][0]), jnp.where(far_half, r[0][1], r[0][0]))
    send_d[:, EX, :] = picked[:, :128]

    def d_send(k, carry):
        who = lax.rem(at + k, PLANE)
        half_, line_ = on_ring(z + reach(core, lax.rem(k // PLANE + mid, runs)))
        dst = line_ * PLANE + who
        pltpu.make_async_remote_copy(
            src_ref=send_d.at[dst, pl.ds(0, EX + 1)], dst_ref=recv_d.at[held, pl.ds(0, EX + 1)],
            send_sem=sd_sem, recv_sem=rd_sem, device_id={"dp": dst, "tensor": y * 2 + half_}, device_id_type=MESH,
        ).start()
        return carry

    lax.fori_loop(0, mid * PLANE, d_send, 0)
    lax.fori_loop(mid * PLANE + 1, n_dp, d_send, 0)
    recv_d[held] = send_d[d]
    owner_half, _ = on_ring(z + mid)
    for p in range(2):
        ev_s[p] = v_ref[p, pl.ds(2 * y + owner_half, EX, stride=8), :]
    ev_copy = pltpu.make_async_remote_copy(
        src_ref=ev_s, dst_ref=ev_r, send_sem=ev_sem.at[0], recv_sem=ev_sem.at[1], device_id=ring_peer(mid), device_id_type=MESH,
    )
    ev_copy.start()
    for i in range(YN):
        @pl.when(y != i)
        def _():
            y_send(i).wait_send()
    seg_copy.wait_send()
    for c in swaps + gathers:
        c.wait_send()
    ev_copy.wait_recv()
    ev_out = pltpu.make_async_copy(ev_r, ev_ref, out_sem.at[0])
    ev_out.start()
    whole = pltpu.make_async_remote_copy(
        src_ref=send_d.at[pl.ds(0, n_dp - 1), pl.ds(0, EX + 1)], dst_ref=recv_d.at[pl.ds(0, n_dp - 1), pl.ds(0, EX + 1)],
        send_sem=sd_sem, recv_sem=rd_sem, device_id=ring_peer(mid), device_id_type=MESH,
    )
    whole.wait_recv()
    rows_t = recv_d[:, EX, :].T
    fisher = jnp.zeros((KP, 128), jnp.float32)
    for e in range(EX):
        fisher += jnp.dot(
            rows_t[e * KP:(e + 1) * KP], recv_d[:, e, :], precision=HIGH, preferred_element_type=jnp.float32
        )
    f_v[0] = fisher * (1.0 / EXAMPLES)
    f_out = pltpu.make_async_copy(f_v, f_ref, out_sem.at[1])
    f_out.start()
    ev_copy.wait_send()
    whole.wait_send()
    ev_out.wait()
    f_out.wait()


def hand_over(ev_ref, f_ref, ev_out, f_out, sem):
    copies = [pltpu.make_async_copy(ev_ref, ev_out, sem.at[0]), pltpu.make_async_copy(f_ref, f_out, sem.at[1])]
    for c in copies:
        c.start()
    for c in copies:
        c.wait()


def shards(xo, go, xu, gu, pxo, pgo, pxu, pgu, seg, owner):
    n_dp = lax.axis_size("dp")
    k1, k2 = xo.shape[1], gu.shape[1]
    bf, f32, i32 = jnp.bfloat16, jnp.float32, jnp.int32
    hbm = pl.BlockSpec(memory_space=pltpu.HBM)
    dma, vm = pltpu.SemaphoreType.DMA, pltpu.VMEM
    outs = (jax.ShapeDtypeStruct((2, EX, 128), f32), jax.ShapeDtypeStruct((1, KP, 128), f32))
    ev, fisher = pl.pallas_call(
        functools.partial(kernel, n_dp),
        out_shape=outs,
        in_specs=[hbm] * 10,
        out_specs=(hbm, hbm),
        scratch_shapes=[
            vm((TOK, k1), bf), vm((TOK, k1), bf), vm((TOK, k1), bf), vm((TOK, k2), bf),
            vm((KP, k1), bf), vm((KP, k1), bf), vm((KP, k1), bf), vm((KP, k2), bf),
            vm((1, TOK), i32), vm((1, owner.shape[0]), i32), vm((2, EX, 128), f32), vm((2, EX, 128), f32), vm((1, KP, 128), f32),
            vm((4, KP, TOK), f32), vm((YN, KP, TOK), f32), vm((1, TOK), i32), vm((KP, TOK), f32), vm((2, KP, TOK), f32),
            vm((4, KP, TOK), f32), vm((128, 128), f32), vm((2, KP, 128), f32), vm((n_dp, 8, 128), f32), vm((n_dp, 8, 128), f32),
            dma((11,)), dma((2,)), dma((4,)), dma((4,)), dma((2,)), dma((2,)), dma((2,)), dma((3,)), dma((4,)), dma((2,)), dma, dma,
        ],
        compiler_params=pltpu.CompilerParams(collective_id=0, has_side_effects=True, vmem_limit_bytes=60 << 20),
    )(xo, go, xu, gu, pxo.T, pgo.T, pxu.T, pgu.T, seg, owner.reshape(1, -1))
    return pl.pallas_call(
        hand_over, out_shape=outs, in_specs=[hbm, hbm], out_specs=(hbm, hbm), scratch_shapes=[dma((2,))],
    )(ev, fisher)


def solution(mesh):
    in_specs = (P("dp", "tensor"),) * 4 + (P("tensor", None),) * 4 + (P("dp", None), P())
    out_specs = (P(None, "dp", "tensor"), P("dp", None, "tensor"))
    return jax.shard_map(shards, mesh=mesh, in_specs=in_specs, out_specs=out_specs, check_vma=False)
```

time: 47.9 us -> 43.6 us (0.910)
  local copies, waits for them, and re-layouts: 2.59 us -> 0 us
  Pallas kernels: 44.4 us -> 42.8 us
    unnamed x2 -> x0, local copies, waits for them, and re-layouts: 2.59 us -> none
    pallas_call x1 -> x2, Pallas kernels: 44.4 us -> 42.8 us  [the longest x1 41.1 us: shards(): pl.pallas_call(functools.partial(kernel, n_dp), out_shape=outs, in_specs=...]
where the time goes in v2:
time: 43.6 us; the launch traced here: 43.5 us
  Pallas kernels  42.8 us (98%)
  between operations  0.64 us (1%)
    pallas_call x1, Pallas kernels, shards(): pl.pallas_call(functools.partial(kernel, n_dp), out_shape=outs, in_specs=...  41.1 us
    pallas_call x1, Pallas kernels, shards(): pl.pallas_call(hand_over, out_shape=outs, in_specs=[hbm, hbm], out_specs=...  1.74 us

profile of v2, /device:TPU:1, one launch (start us, length us, event | category | flops | bytes accessed | tf_op | source)
XLA Modules:
  0.0 43.5 jit_solution(12437666405084444426)
XLA Ops:
  0.6 41.1 %shard_map.113 = (f32[2,4,128]{2,1,0:T(4,128)}, f32[1,32,128]{2,1,0:T(8,128)}) custom-call(bf16[256,1024]{1,0:T(8,128)(2,1)} %xo_ref.1, bf16[256,1024]{1,0:T(8,128)(2,1)} %go_ref.1, bf16[256,1024]{1,0:T(8,128)(2,1)} %xu_ref.1, bf16[256,3584]{1,0:T(8,128)(2,1)} %gu_ref.1, bf16[32,1024]{1,0:T(8,128)(2,1)} %bitcast.6, bf16[32,1024]{1,0:T(8,128)(2,1)} %bitcast.7, ...), custom_call_target="tpu_custom_call" | custom-call | tf_op jit(solution)/shard_map/pallas_call | solution.py:249
  41.7 1.7 %shard_map.114 = (f32[2,4,128]{2,1,0:T(4,128)}, f32[1,32,128]{2,1,0:T(8,128)}) custom-call(f32[2,4,128]{2,1,0:T(4,128)} %get-tuple-element.4.ev_ref, f32[1,32,128]{2,1,0:T(8,128)} %get-tuple-element.5.f_ref), custom_call_target="tpu_custom_call" | custom-call | tf_op jit(solution)/shard_map/pallas_call | solution.py:264

commit v3 on v2

--- a/solution.py
+++ b/solution.py
@@ -24,9 +24,9 @@
     n_dp,
     xo_ref, go_ref, xu_ref, gu_ref, pxo_ref, pgo_ref, pxu_ref, pgu_ref, seg_ref, own_ref,
     ev_ref, f_ref,
-    xo, go, xu, gu, pxo, pgo, pxu, pgu, seg_v, own_v, ev_s, ev_r, f_v,
+    xo, go, xu, gu, pxo, pgo, pxu, pgu, seg_v, own_v, ev_s, ev_r,
     part, recv_y, seg_r, sum_z, recv_z, full, g_ref, v_ref, send_d, recv_d,
-    in_sem, out_sem, sy_sem, ry_sem, seg_sem, sz_sem, rz_sem, sg_sem, rg_sem, ev_sem, sd_sem, rd_sem,
+    in_sem, sy_sem, ry_sem, seg_sem, sz_sem, rz_sem, sg_sem, rg_sem, ev_sem, sd_sem, rd_sem, met_sem, known_sem,
 ):
     d = lax.axis_index("dp")
     t = lax.axis_index("tensor")
@@ -65,17 +65,12 @@
         c.start()
 
     barrier = pltpu.get_barrier_semaphore()
-
-    def greet(k, carry):
-        who = lax.rem(at + k, PLANE)
-        half_, line = on_ring(z - reach(lax.rem(who, 2), k // PLANE))
-        pl.semaphore_signal(barrier, inc=1, device_id={"dp": line * PLANE + who, "tensor": y * 2 + half_}, device_id_type=MESH)
-        return carry
-
-    lax.fori_loop(1, n_dp, greet, 0)
-    for step in (mid, -mid):
+    near = (2, -2, 1, -1)
+    for k in (4, 5, 3, 2, 6, 7, 1):
+        pl.semaphore_signal(barrier, inc=1, device_id={"dp": plane * PLANE + lax.rem(at + k, PLANE)}, device_id_type=MESH)
+    for step in near:
         pl.semaphore_signal(barrier, inc=1, device_id=ring_peer(step), device_id_type=MESH)
-    for j in range(1, YN):
+    for j in (2, 1, 3):
         pl.semaphore_signal(barrier, inc=1, device_id={"tensor": y_peer(j) * 2 + zh}, device_id_type=MESH)
 
     def project(w, x):
@@ -102,17 +97,14 @@
             copies[8].wait()
             part[i, :, pl.ds(half, half)] = project(w[...], x[pl.ds(half, half), :])
         if i == 2:
-            pl.semaphore_wait(barrier, n_dp - 1 + 2 + YN - 1)
+            pl.semaphore_wait(barrier, PLANE - 1 + len(near) + YN - 1)
             for k in range(3):
                 y_start(k)
     y_start(3)
+    for step in near:
+        pl.semaphore_signal(met_sem, inc=1, device_id=ring_peer(step), device_id_type=MESH)
     copies[9].wait()
     copies[10].wait()
-    seg_copy = pltpu.make_async_remote_copy(
-        src_ref=seg_v, dst_ref=seg_r, send_sem=seg_sem.at[0], recv_sem=seg_sem.at[1], device_id=ring_peer(mid), device_id_type=MESH,
-    )
-    seg_copy.start()
-
     total = part[y]
     for j in range(1, YN):
         p = y_peer(j)
@@ -122,6 +114,7 @@
         ).wait_recv()
         total += recv_y[p]
     sum_z[...] = total
+    pl.semaphore_wait(met_sem, len(near))
     swaps = [
         pltpu.make_async_remote_copy(
             src_ref=sum_z, dst_ref=recv_z.at[i], send_sem=sz_sem.at[i], recv_sem=rz_sem.at[i],
@@ -131,6 +124,12 @@
     ]
     for c in swaps:
         c.start()
+    for step in near[:2]:
+        pl.semaphore_signal(known_sem, inc=1, device_id=ring_peer(step), device_id_type=MESH)
+    seg_copy = pltpu.make_async_remote_copy(
+        src_ref=seg_v, dst_ref=seg_r, send_sem=seg_sem.at[0], recv_sem=seg_sem.at[1], device_id=ring_peer(mid), device_id_type=MESH,
+    )
+    seg_copy.start()
     for c in swaps:
         c.wait_recv()
     full[y] = recv_z[0] + recv_z[1]
@@ -181,18 +180,22 @@
         send_d[:, e, :] = jnp.where(is_up, jnp.where(far_half, r[1][1], r[1][0]), jnp.where(far_half, r[0][1], r[0][0]))
     send_d[:, EX, :] = picked[:, :128]
 
-    def d_send(k, carry):
-        who = lax.rem(at + k, PLANE)
-        half_, line_ = on_ring(z + reach(core, lax.rem(k // PLANE + mid, runs)))
+    def d_send(k):
+        who = lax.rem(at + k % PLANE, PLANE)
+        half_, line_ = on_ring(z + reach(core, k // PLANE))
         dst = line_ * PLANE + who
         pltpu.make_async_remote_copy(
             src_ref=send_d.at[dst, pl.ds(0, EX + 1)], dst_ref=recv_d.at[held, pl.ds(0, EX + 1)],
             send_sem=sd_sem, recv_sem=rd_sem, device_id={"dp": dst, "tensor": y * 2 + half_}, device_id_type=MESH,
         ).start()
-        return carry
-
-    lax.fori_loop(0, mid * PLANE, d_send, 0)
-    lax.fori_loop(mid * PLANE + 1, n_dp, d_send, 0)
+
+    pl.semaphore_wait(known_sem, 2)
+
+    def hops(k):
+        return min(k // PLANE, runs - k // PLANE) + min(k % PLANE, PLANE - k % PLANE) // 2
+
+    for k in sorted(range(1, n_dp), key=hops, reverse=True):
+        d_send(k)
     recv_d[held] = send_d[d]
     owner_half, _ = on_ring(z + mid)
     for p in range(2):
@@ -208,9 +211,6 @@
     seg_copy.wait_send()
     for c in swaps + gathers:
         c.wait_send()
-    ev_copy.wait_recv()
-    ev_out = pltpu.make_async_copy(ev_r, ev_ref, out_sem.at[0])
-    ev_out.start()
     whole = pltpu.make_async_remote_copy(
         src_ref=send_d.at[pl.ds(0, n_dp - 1), pl.ds(0, EX + 1)], dst_ref=recv_d.at[pl.ds(0, n_dp - 1), pl.ds(0, EX + 1)],
         send_sem=sd_sem, recv_sem=rd_sem, device_id=ring_peer(mid), device_id_type=MESH,
@@ -222,13 +222,10 @@
         fisher += jnp.dot(
             rows_t[e * KP:(e + 1) * KP], recv_d[:, e, :], precision=HIGH, preferred_element_type=jnp.float32
         )
-    f_v[0] = fisher * (1.0 / EXAMPLES)
-    f_out = pltpu.make_async_copy(f_v, f_ref, out_sem.at[1])
-    f_out.start()
-    ev_copy.wait_send()
+    f_ref[0] = fisher * (1.0 / EXAMPLES)
+    ev_copy.wait()
+    ev_ref[...] = ev_r[...]
     whole.wait_send()
-    ev_out.wait()
-    f_out.wait()
 
 
 def hand_over(ev_ref, f_ref, ev_out, f_out, sem):
@@ -243,26 +240,29 @@
     n_dp = lax.axis_size("dp")
     k1, k2 = xo.shape[1], gu.shape[1]
     bf, f32, i32 = jnp.bfloat16, jnp.float32, jnp.int32
-    hbm = pl.BlockSpec(memory_space=pltpu.HBM)
+    hbm, vmem = pl.BlockSpec(memory_space=pltpu.HBM), pl.BlockSpec(memory_space=pltpu.VMEM)
     dma, vm = pltpu.SemaphoreType.DMA, pltpu.VMEM
     outs = (jax.ShapeDtypeStruct((2, EX, 128), f32), jax.ShapeDtypeStruct((1, KP, 128), f32))
+    args = (xo, go, xu, gu, pxo.T, pgo.T, pxu.T, pgu.T, seg, owner.reshape(1, -1))
     ev, fisher = pl.pallas_call(
         functools.partial(kernel, n_dp),
         out_shape=outs,
         in_specs=[hbm] * 10,
-        out_specs=(hbm, hbm),
+        out_specs=(vmem, vmem),
         scratch_shapes=[
             vm((TOK, k1), bf), vm((TOK, k1), bf), vm((TOK, k1), bf), vm((TOK, k2), bf),
             vm((KP, k1), bf), vm((KP, k1), bf), vm((KP, k1), bf), vm((KP, k2), bf),
-            vm((1, TOK), i32), vm((1, owner.shape[0]), i32), vm((2, EX, 128), f32), vm((2, EX, 128), f32), vm((1, KP, 128), f32),
+            vm((1, TOK), i32), vm((1, owner.shape[0]), i32), vm((2, EX, 128), f32), vm((2, EX, 128), f32),
             vm((4, KP, TOK), f32), vm((YN, KP, TOK), f32), vm((1, TOK), i32), vm((KP, TOK), f32), vm((2, KP, TOK), f32),
             vm((4, KP, TOK), f32), vm((128, 128), f32), vm((2, KP, 128), f32), vm((n_dp, 8, 128), f32), vm((n_dp, 8, 128), f32),
-            dma((11,)), dma((2,)), dma((4,)), dma((4,)), dma((2,)), dma((2,)), dma((2,)), dma((3,)), dma((4,)), dma((2,)), dma, dma,
+            dma((11,)), dma((4,)), dma((4,)), dma((2,)), dma((2,)), dma((2,)), dma((3,)), dma((4,)), dma((2,)), dma, dma,
+            pltpu.SemaphoreType.REGULAR, pltpu.SemaphoreType.REGULAR,
         ],
-        compiler_params=pltpu.CompilerParams(collective_id=0, has_side_effects=True, vmem_limit_bytes=60 << 20),
-    )(xo, go, xu, gu, pxo.T, pgo.T, pxu.T, pgu.T, seg, owner.reshape(1, -1))
+        compiler_params=pltpu.CompilerParams(collective_id=0, has_side_effects=True, vmem_limit_bytes=32 << 20),
+    )(*(pltpu.with_memory_space_constraint(a, pltpu.HBM) for a in args))
     return pl.pallas_call(
-        hand_over, out_shape=outs, in_specs=[hbm, hbm], out_specs=(hbm, hbm), scratch_shapes=[dma((2,))],
+        hand_over, out_shape=outs, in_specs=[vmem, vmem], out_specs=(hbm, hbm), scratch_shapes=[dma((2,))],
+        compiler_params=pltpu.CompilerParams(vmem_limit_bytes=4 << 20),
     )(ev, fisher)
 
 

time: 43.6 us -> 38.4 us (0.88)
  Pallas kernels: 42.8 us -> 37.6 us
    pallas_call x1, Pallas kernels: 41.1 us -> 37 us  [shards(): pl.pallas_call(functools.partial(kernel, n_dp), out_shape=outs, in_specs=...]
    pallas_call x1, Pallas kernels: 1.74 us -> 0.63 us  [shards(): pl.pallas_call(hand_over, out_shape=outs, in_specs=[vmem, vmem], out_spec...]
where the time goes in v3:
time: 38.4 us; the launch traced here: 38.3 us
  Pallas kernels  37.6 us (98%)
  between operations  0.64 us (2%)
    pallas_call x1, Pallas kernels, shards(): pl.pallas_call(functools.partial(kernel, n_dp), out_shape=outs, in_specs=...  37 us

profile of v3, /device:TPU:1, one launch (start us, length us, event | category | flops | bytes accessed | tf_op | source)
XLA Modules:
  0.0 38.3 jit_solution(13259879707282697276)
XLA Ops:
  0.6 37.0 %shard_map.113 = (f32[2,4,128]{2,1,0:T(4,128)S(1)}, f32[1,32,128]{2,1,0:T(8,128)S(1)}) custom-call(bf16[256,1024]{1,0:T(8,128)(2,1)} %xo_ref.1, bf16[256,1024]{1,0:T(8,128)(2,1)} %go_ref.1, bf16[256,1024]{1,0:T(8,128)(2,1)} %xu_ref.1, bf16[256,3584]{1,0:T(8,128)(2,1)} %gu_ref.1, bf16[32,1024]{1,0:T(8,128)(2,1)} %bitcast.6, bf16[32,1024]{1,0:T(8,128)(2,1)} %bitcast.7, ...), custom_call_target="tpu_custom_call" | custom-call | tf_op jit(solution)/shard_map/pallas_call | solution.py:247
  37.6 0.6 %shard_map.114 = (f32[2,4,128]{2,1,0:T(4,128)}, f32[1,32,128]{2,1,0:T(8,128)}) custom-call(f32[2,4,128]{2,1,0:T(4,128)S(1)} %get-tuple-element.4.ev_ref, f32[1,32,128]{2,1,0:T(8,128)S(1)} %get-tuple-element.5.f_ref), custom_call_target="tpu_custom_call" | custom-call | tf_op jit(solution)/shard_map/pallas_call | solution.py:263

commit v4 on v3

--- a/solution.py
+++ b/solution.py
@@ -18,6 +18,20 @@
 MESH = pl.DeviceIdType.MESH
 NT = (((1,), (1,)), ((), ()))
 TN = (((0,), (0,)), ((), ()))
+
+
+def split(x):
+    top = x.astype(jnp.bfloat16)
+    return top, (x - top.astype(jnp.float32)).astype(jnp.bfloat16)
+
+
+def dot3(a, b, dims):
+    (a1, a2), (b1, b2) = split(a), split(b)
+
+    def one(p, q):
+        return lax.dot_general(p, q, dims, preferred_element_type=jnp.float32)
+
+    return one(a1, b1) + (one(a1, b2) + one(a2, b1))
 
 
 def kernel(
@@ -146,7 +160,7 @@
     seg = seg_r[...]
     scale = (EX / TOK) ** 0.5
     masks = [jnp.where(seg == e, scale, 0.0).astype(jnp.float32) for e in range(EX)]
-    onehot = (lax.broadcasted_iota(jnp.int32, (BLOCKS, n_dp), 0) == own_v[...]).astype(jnp.float32)
+    onehot = (lax.broadcasted_iota(jnp.int32, (BLOCKS, n_dp), 0) == own_v[...]).astype(jnp.bfloat16)
     for j in range(1, YN):
         p = y_peer(j)
         pltpu.make_async_remote_copy(
@@ -161,15 +175,15 @@
         high_e = jnp.concatenate([high * m for m in masks], axis=0)
         low_e = jnp.concatenate([low * m for m in masks], axis=0)
         low_4 = jnp.concatenate([low] * 4, axis=0)
-        g_ref[...] = lax.dot_general(high_e, low_4, NT, precision=HIGH, preferred_element_type=jnp.float32)
+        g_ref[...] = dot3(high_e, low_4, NT)
         rows = [g_ref[pl.ds(j, EX * KP // 4, stride=4), :] for j in range(4)]
         v_ref[p] = jnp.where(group == 0, rows[0], jnp.where(group == 1, rows[1], jnp.where(group == 2, rows[2], rows[3])))
-        by_block.append(lax.dot_general(high, low_e, NT, precision=HIGH, preferred_element_type=jnp.float32))
+        by_block.append(dot3(high, low_e, NT))
 
     table = jnp.concatenate(
         [jnp.concatenate(by_block, axis=0), (lax.broadcasted_iota(jnp.int32, (BLOCKS, 128), 0) >= KP).astype(jnp.float32)], axis=1
     )
-    picked = lax.dot_general(onehot, table, TN, precision=HIGH, preferred_element_type=jnp.float32)
+    picked = sum(lax.dot_general(onehot, part_, TN, preferred_element_type=jnp.float32) for part_ in split(table))
     is_up = picked[:, 128:] > 0.5
     low = mid - 1 + core
     line = lax.broadcasted_iota(jnp.int32, (n_dp, 128), 0) // PLANE
@@ -194,9 +208,6 @@
     def hops(k):
         return min(k // PLANE, runs - k // PLANE) + min(k % PLANE, PLANE - k % PLANE) // 2
 
-    for k in sorted(range(1, n_dp), key=hops, reverse=True):
-        d_send(k)
-    recv_d[held] = send_d[d]
     owner_half, _ = on_ring(z + mid)
     for p in range(2):
         ev_s[p] = v_ref[p, pl.ds(2 * y + owner_half, EX, stride=8), :]
@@ -204,6 +215,10 @@
         src_ref=ev_s, dst_ref=ev_r, send_sem=ev_sem.at[0], recv_sem=ev_sem.at[1], device_id=ring_peer(mid), device_id_type=MESH,
     )
     ev_copy.start()
+
+    for k in sorted(range(1, n_dp), key=hops, reverse=True):
+        d_send(k)
+    recv_d[held] = send_d[d]
     for i in range(YN):
         @pl.when(y != i)
         def _():
@@ -219,9 +234,7 @@
     rows_t = recv_d[:, EX, :].T
     fisher = jnp.zeros((KP, 128), jnp.float32)
     for e in range(EX):
-        fisher += jnp.dot(
-            rows_t[e * KP:(e + 1) * KP], recv_d[:, e, :], precision=HIGH, preferred_element_type=jnp.float32
-        )
+        fisher += dot3(rows_t[e * KP:(e + 1) * KP], recv_d[:, e, :], (((1,), (0,)), ((), ())))
     f_ref[0] = fisher * (1.0 / EXAMPLES)
     ev_copy.wait()
     ev_ref[...] = ev_r[...]

time: 38.4 us -> 37.4 us (0.974)
  Pallas kernels: 37.6 us -> 36.6 us
    pallas_call x1, Pallas kernels: 37 us -> 36 us  [shards(): pl.pallas_call(functools.partial(kernel, n_dp), out_shape=outs, in_specs=...]
where the time goes in v4:
time: 37.4 us; the launch traced here: 37.3 us
  Pallas kernels  36.6 us (98%)
  between operations  0.64 us (2%)
    pallas_call x1, Pallas kernels, shards(): pl.pallas_call(functools.partial(kernel, n_dp), out_shape=outs, in_specs=...  36 us

profile of v4, /device:TPU:1, one launch (start us, length us, event | category | flops | bytes accessed | tf_op | source)
XLA Modules:
  0.0 37.3 jit_solution(3565788543531434042)
XLA Ops:
  0.6 36.0 %shard_map.113 = (f32[2,4,128]{2,1,0:T(4,128)S(1)}, f32[1,32,128]{2,1,0:T(8,128)S(1)}) custom-call(bf16[256,1024]{1,0:T(8,128)(2,1)} %xo_ref.1, bf16[256,1024]{1,0:T(8,128)(2,1)} %go_ref.1, bf16[256,1024]{1,0:T(8,128)(2,1)} %xu_ref.1, bf16[256,3584]{1,0:T(8,128)(2,1)} %gu_ref.1, bf16[32,1024]{1,0:T(8,128)(2,1)} %bitcast.6, bf16[32,1024]{1,0:T(8,128)(2,1)} %bitcast.7, ...), custom_call_target="tpu_custom_call" | custom-call | tf_op jit(solution)/shard_map/pallas_call | solution.py:260
  36.6 0.6 %shard_map.114 = (f32[2,4,128]{2,1,0:T(4,128)}, f32[1,32,128]{2,1,0:T(8,128)}) custom-call(f32[2,4,128]{2,1,0:T(4,128)S(1)} %get-tuple-element.4.ev_ref, f32[1,32,128]{2,1,0:T(8,128)S(1)} %get-tuple-element.5.f_ref), custom_call_target="tpu_custom_call" | custom-call | tf_op jit(solution)/shard_map/pallas_call | solution.py:276

commit v5 on v4

--- a/solution.py
+++ b/solution.py
@@ -14,7 +14,6 @@
 EXAMPLES = 256
 YN = 4
 PLANE = 8
-HIGH = lax.Precision.HIGHEST
 MESH = pl.DeviceIdType.MESH
 NT = (((1,), (1,)), ((), ()))
 TN = (((0,), (0,)), ((), ()))
@@ -26,7 +25,7 @@
 
 
 def dot3(a, b, dims):
-    (a1, a2), (b1, b2) = split(a), split(b)
+    (a1, a2), (b1, b2) = a, b
 
     def one(p, q):
         return lax.dot_general(p, q, dims, preferred_element_type=jnp.float32)
@@ -90,109 +89,121 @@
     def project(w, x):
         return lax.dot_general(w, x, NT, preferred_element_type=jnp.float32)
 
-    def y_send(i):
+    def y_send(i, h):
         return pltpu.make_async_remote_copy(
-            src_ref=part.at[i], dst_ref=recv_y.at[y], send_sem=sy_sem.at[i], recv_sem=ry_sem.at[y],
+            src_ref=part.at[i, h], dst_ref=recv_y.at[y, h], send_sem=sy_sem.at[i, h], recv_sem=ry_sem.at[y, h],
             device_id={"tensor": i * 2 + zh}, device_id_type=MESH,
         )
 
-    def y_start(i):
+    def y_start(i, h):
         @pl.when(y != i)
         def _():
-            y_send(i).start()
-
-    for i, (w, x) in enumerate(((pxo, xo), (pgo, go), (pxu, xu), (pgu, gu))):
+            y_send(i, h).start()
+
+    for i, (w, x) in enumerate(((pxo, xo), (pgo, go), (pxu, xu))):
         copies[2 * i].wait()
         copies[2 * i + 1].wait()
-        if i < 3:
-            part[i] = project(w[...], x[...])
-        else:
-            part[i, :, pl.ds(0, half)] = project(w[...], x[pl.ds(0, half), :])
-            copies[8].wait()
-            part[i, :, pl.ds(half, half)] = project(w[...], x[pl.ds(half, half), :])
-        if i == 2:
-            pl.semaphore_wait(barrier, PLANE - 1 + len(near) + YN - 1)
-            for k in range(3):
-                y_start(k)
-    y_start(3)
+        q = project(w[...], x[...])
+        part[i, 0] = q[:, :half]
+        part[i, 1] = q[:, half:]
+    pl.semaphore_wait(barrier, PLANE - 1 + len(near) + YN - 1)
+    for h in range(2):
+        for i in range(3):
+            y_start(i, h)
+    copies[6].wait()
+    for h in range(2):
+        copies[7 + h].wait()
+        part[3, h] = project(pgu[...], gu[pl.ds(h * half, half), :])
+        y_start(3, h)
     for step in near:
         pl.semaphore_signal(met_sem, inc=1, device_id=ring_peer(step), device_id_type=MESH)
     copies[9].wait()
     copies[10].wait()
-    total = part[y]
-    for j in range(1, YN):
-        p = y_peer(j)
-        pltpu.make_async_remote_copy(
-            src_ref=part.at[p], dst_ref=recv_y.at[p], send_sem=sy_sem.at[p], recv_sem=ry_sem.at[p],
-            device_id={"tensor": p * 2 + zh}, device_id_type=MESH,
-        ).wait_recv()
-        total += recv_y[p]
-    sum_z[...] = total
-    pl.semaphore_wait(met_sem, len(near))
-    swaps = [
-        pltpu.make_async_remote_copy(
-            src_ref=sum_z, dst_ref=recv_z.at[i], send_sem=sz_sem.at[i], recv_sem=rz_sem.at[i],
-            device_id=ring_peer(step), device_id_type=MESH,
-        )
-        for i, step in enumerate((mid, -mid))
-    ]
-    for c in swaps:
-        c.start()
+
+    swaps = []
+    for h in range(2):
+        total = part[y, h]
+        for j in range(1, YN):
+            p = y_peer(j)
+            pltpu.make_async_remote_copy(
+                src_ref=part.at[p, h], dst_ref=recv_y.at[p, h], send_sem=sy_sem.at[p, h], recv_sem=ry_sem.at[p, h],
+                device_id={"tensor": p * 2 + zh}, device_id_type=MESH,
+            ).wait_recv()
+            total += recv_y[p, h]
+        sum_z[h] = total
+        if h == 0:
+            pl.semaphore_wait(met_sem, len(near))
+        swaps.append([
+            pltpu.make_async_remote_copy(
+                src_ref=sum_z.at[h], dst_ref=recv_z.at[i, h], send_sem=sz_sem.at[i, h], recv_sem=rz_sem.at[i, h],
+                device_id=ring_peer(step), device_id_type=MESH,
+            )
+            for i, step in enumerate((mid, -mid))
+        ])
+        for c in swaps[h]:
+            c.start()
     for step in near[:2]:
         pl.semaphore_signal(known_sem, inc=1, device_id=ring_peer(step), device_id_type=MESH)
     seg_copy = pltpu.make_async_remote_copy(
         src_ref=seg_v, dst_ref=seg_r, send_sem=seg_sem.at[0], recv_sem=seg_sem.at[1], device_id=ring_peer(mid), device_id_type=MESH,
     )
     seg_copy.start()
-    for c in swaps:
-        c.wait_recv()
-    full[y] = recv_z[0] + recv_z[1]
     gathers = []
-    for j in range(1, YN):
-        p = y_peer(j)
-        c = pltpu.make_async_remote_copy(
-            src_ref=full.at[y], dst_ref=full.at[y], send_sem=sg_sem.at[j - 1], recv_sem=rg_sem.at[y],
-            device_id={"tensor": p * 2 + zh}, device_id_type=MESH,
-        )
-        c.start()
-        gathers.append(c)
+    for h in range(2):
+        for c in swaps[h]:
+            c.wait_recv()
+        full[y, h] = recv_z[0, h] + recv_z[1, h]
+        for j in (2, 1, 3):
+            p = y_peer(j)
+            c = pltpu.make_async_remote_copy(
+                src_ref=full.at[y, h], dst_ref=full.at[y, h], send_sem=sg_sem.at[j - 1, h], recv_sem=rg_sem.at[y, h],
+                device_id={"tensor": p * 2 + zh}, device_id_type=MESH,
+            )
+            c.start()
+            gathers.append(c)
     seg_copy.wait_recv()
     seg = seg_r[...]
     scale = (EX / TOK) ** 0.5
-    masks = [jnp.where(seg == e, scale, 0.0).astype(jnp.float32) for e in range(EX)]
+    masks = [jnp.where(seg == e, scale, 0.0).astype(jnp.bfloat16) for e in range(EX)]
     onehot = (lax.broadcasted_iota(jnp.int32, (BLOCKS, n_dp), 0) == own_v[...]).astype(jnp.bfloat16)
-    for j in range(1, YN):
-        p = y_peer(j)
-        pltpu.make_async_remote_copy(
-            src_ref=full.at[p], dst_ref=full.at[p], send_sem=sg_sem.at[j - 1], recv_sem=rg_sem.at[p],
-            device_id={"tensor": p * 2 + zh}, device_id_type=MESH,
-        ).wait_recv()
-
-    group = lax.broadcasted_iota(jnp.int32, (EX * KP // 4, 128), 1) // KP
-    by_block = []
-    for p in range(2):
-        low, high = full[2 * p], full[2 * p + 1]
-        high_e = jnp.concatenate([high * m for m in masks], axis=0)
-        low_e = jnp.concatenate([low * m for m in masks], axis=0)
-        low_4 = jnp.concatenate([low] * 4, axis=0)
-        g_ref[...] = dot3(high_e, low_4, NT)
-        rows = [g_ref[pl.ds(j, EX * KP // 4, stride=4), :] for j in range(4)]
-        v_ref[p] = jnp.where(group == 0, rows[0], jnp.where(group == 1, rows[1], jnp.where(group == 2, rows[2], rows[3])))
-        by_block.append(dot3(high, low_e, NT))
-
-    table = jnp.concatenate(
-        [jnp.concatenate(by_block, axis=0), (lax.broadcasted_iota(jnp.int32, (BLOCKS, 128), 0) >= KP).astype(jnp.float32)], axis=1
-    )
-    picked = sum(lax.dot_general(onehot, part_, TN, preferred_element_type=jnp.float32) for part_ in split(table))
-    is_up = picked[:, 128:] > 0.5
+    block_is_up = (lax.broadcasted_iota(jnp.int32, (BLOCKS, 128), 0) >= KP).astype(jnp.bfloat16)
+    is_up = lax.dot_general(onehot, block_is_up, TN, preferred_element_type=jnp.float32) > 0.5
     low = mid - 1 + core
     line = lax.broadcasted_iota(jnp.int32, (n_dp, 128), 0) // PLANE
     pos = z + lax.rem(line - z + low + ring, runs) - low
     far_half = lax.rem(pos + ring, ring) >= runs
+    group = lax.broadcasted_iota(jnp.int32, (EX * KP // 4, 128), 1) // KP
+
+    def by_group(rows):
+        return jnp.where(group == 0, rows[0], jnp.where(group == 1, rows[1], jnp.where(group == 2, rows[2], rows[3])))
+
+    outer = [0.0, 0.0]
+    for h in range(2):
+        for j in range(1, YN):
+            p = y_peer(j)
+            pltpu.make_async_remote_copy(
+                src_ref=full.at[p, h], dst_ref=full.at[p, h], send_sem=sg_sem.at[j - 1, h], recv_sem=rg_sem.at[p, h],
+                device_id={"tensor": p * 2 + zh}, device_id_type=MESH,
+            ).wait_recv()
+        m_h = [m[:, h * half:(h + 1) * half] for m in masks]
+        for p in range(2):
+            low, high = split(full[2 * p, h]), split(full[2 * p + 1, h])
+            low_4 = [jnp.concatenate([v] * 4, axis=0) for v in low]
+            high_e = [jnp.concatenate([v * m for m in m_h], axis=0) for v in high]
+            outer[p] += dot3(high_e, low_4, NT)
+
+    by_block = []
+    for p in range(2):
+        g_ref[...] = outer[p]
+        v_ref[p] = by_group([g_ref[pl.ds(j, EX * KP // 4, stride=4), :] for j in range(4)])
+        by_block.append(by_group([outer[p][e * KP:(e + 1) * KP] for e in range(EX)]))
+
+    table = split(jnp.concatenate(by_block, axis=0))
+    picked = sum(lax.dot_general(onehot, v, TN, preferred_element_type=jnp.float32) for v in table)
     for e in range(EX):
         r = [[jnp.broadcast_to(v_ref[p, pl.ds(2 * y + h + 8 * e, 1), :], (n_dp, 128)) for h in range(2)] for p in range(2)]
         send_d[:, e, :] = jnp.where(is_up, jnp.where(far_half, r[1][1], r[1][0]), jnp.where(far_half, r[0][1], r[0][0]))
-    send_d[:, EX, :] = picked[:, :128]
+    send_d[:, EX, :] = picked
 
     def d_send(k):
         who = lax.rem(at + k % PLANE, PLANE)
@@ -222,9 +233,10 @@
     for i in range(YN):
         @pl.when(y != i)
         def _():
-            y_send(i).wait_send()
+            for h in range(2):
+                y_send(i, h).wait_send()
     seg_copy.wait_send()
-    for c in swaps + gathers:
+    for c in swaps[0] + swaps[1] + gathers:
         c.wait_send()
     whole = pltpu.make_async_remote_copy(
         src_ref=send_d.at[pl.ds(0, n_dp - 1), pl.ds(0, EX + 1)], dst_ref=recv_d.at[pl.ds(0, n_dp - 1), pl.ds(0, EX + 1)],
@@ -232,9 +244,9 @@
     )
     whole.wait_recv()
     rows_t = recv_d[:, EX, :].T
-    fisher = jnp.zeros((KP, 128), jnp.float32)
-    for e in range(EX):
-        fisher += dot3(rows_t[e * KP:(e + 1) * KP], recv_d[:, e, :], (((1,), (0,)), ((), ())))
+    left = jnp.concatenate([rows_t[e * KP:(e + 1) * KP] for e in range(EX)], axis=1)
+    right = jnp.concatenate([recv_d[:, e, :] for e in range(EX)], axis=0)
+    fisher = dot3(split(left), split(right), (((1,), (0,)), ((), ())))
     f_ref[0] = fisher * (1.0 / EXAMPLES)
     ev_copy.wait()
     ev_ref[...] = ev_r[...]
@@ -266,9 +278,9 @@
             vm((TOK, k1), bf), vm((TOK, k1), bf), vm((TOK, k1), bf), vm((TOK, k2), bf),
             vm((KP, k1), bf), vm((KP, k1), bf), vm((KP, k1), bf), vm((KP, k2), bf),
             vm((1, TOK), i32), vm((1, owner.shape[0]), i32), vm((2, EX, 128), f32), vm((2, EX, 128), f32),
-            vm((4, KP, TOK), f32), vm((YN, KP, TOK), f32), vm((1, TOK), i32), vm((KP, TOK), f32), vm((2, KP, TOK), f32),
-            vm((4, KP, TOK), f32), vm((128, 128), f32), vm((2, KP, 128), f32), vm((n_dp, 8, 128), f32), vm((n_dp, 8, 128), f32),
-            dma((11,)), dma((4,)), dma((4,)), dma((2,)), dma((2,)), dma((2,)), dma((3,)), dma((4,)), dma((2,)), dma, dma,
+            vm((4, 2, KP, TOK // 2), f32), vm((YN, 2, KP, TOK // 2), f32), vm((1, TOK), i32), vm((2, KP, TOK // 2), f32), vm((2, 2, KP, TOK // 2), f32),
+            vm((4, 2, KP, TOK // 2), f32), vm((128, 128), f32), vm((2, KP, 128), f32), vm((n_dp, 8, 128), f32), vm((n_dp, 8, 128), f32),
+            dma((11,)), dma((4, 2)), dma((4, 2)), dma((2,)), dma((2, 2)), dma((2, 2)), dma((3, 2)), dma((4, 2)), dma((2,)), dma, dma,
             pltpu.SemaphoreType.REGULAR, pltpu.SemaphoreType.REGULAR,
         ],
         compiler_params=pltpu.CompilerParams(collective_id=0, has_side_effects=True, vmem_limit_bytes=32 << 20),

time: 37.4 us -> 37.1 us (level)
  no operation moved by 1% of the time
where the time goes in v5:
time: 37.1 us; the launch traced here: 37 us
  Pallas kernels  36.4 us (98%)
  between operations  0.64 us (2%)
    pallas_call x1, Pallas kernels, shards(): pl.pallas_call(functools.partial(kernel, n_dp), out_shape=outs, in_specs=...  35.8 us

profile of v5, /device:TPU:1, one launch (start us, length us, event | category | flops | bytes accessed | tf_op | source)
XLA Modules:
  0.0 37.0 jit_solution(431037968999753204)
XLA Ops:
  0.6 35.8 %shard_map.113 = (f32[2,4,128]{2,1,0:T(4,128)S(1)}, f32[1,32,128]{2,1,0:T(8,128)S(1)}) custom-call(bf16[256,1024]{1,0:T(8,128)(2,1)} %xo_ref.1, bf16[256,1024]{1,0:T(8,128)(2,1)} %go_ref.1, bf16[256,1024]{1,0:T(8,128)(2,1)} %xu_ref.1, bf16[256,3584]{1,0:T(8,128)(2,1)} %gu_ref.1, bf16[32,1024]{1,0:T(8,128)(2,1)} %bitcast.6, bf16[32,1024]{1,0:T(8,128)(2,1)} %bitcast.7, ...), custom_call_target="tpu_custom_call" | custom-call | tf_op jit(solution)/shard_map/pallas_call | solution.py:272
  36.4 0.6 %shard_map.114 = (f32[2,4,128]{2,1,0:T(4,128)}, f32[1,32,128]{2,1,0:T(8,128)}) custom-call(f32[2,4,128]{2,1,0:T(4,128)S(1)} %get-tuple-element.4.ev_ref, f32[1,32,128]{2,1,0:T(8,128)S(1)} %get-tuple-element.5.f_ref), custom_call_target="tpu_custom_call" | custom-call | tf_op jit(solution)/shard_map/pallas_call | solution.py:288

commit v6 on v5

--- a/solution.py
+++ b/solution.py
@@ -79,12 +79,12 @@
 
     barrier = pltpu.get_barrier_semaphore()
     near = (2, -2, 1, -1)
+    for j in (2, 1, 3):
+        pl.semaphore_signal(barrier, inc=1, device_id={"tensor": y_peer(j) * 2 + zh}, device_id_type=MESH)
     for k in (4, 5, 3, 2, 6, 7, 1):
         pl.semaphore_signal(barrier, inc=1, device_id={"dp": plane * PLANE + lax.rem(at + k, PLANE)}, device_id_type=MESH)
     for step in near:
         pl.semaphore_signal(barrier, inc=1, device_id=ring_peer(step), device_id_type=MESH)
-    for j in (2, 1, 3):
-        pl.semaphore_signal(barrier, inc=1, device_id={"tensor": y_peer(j) * 2 + zh}, device_id_type=MESH)
 
     def project(w, x):
         return lax.dot_general(w, x, NT, preferred_element_type=jnp.float32)
@@ -110,13 +110,13 @@
     for h in range(2):
         for i in range(3):
             y_start(i, h)
+    for step in near:
+        pl.semaphore_signal(met_sem, inc=1, device_id=ring_peer(step), device_id_type=MESH)
     copies[6].wait()
     for h in range(2):
         copies[7 + h].wait()
         part[3, h] = project(pgu[...], gu[pl.ds(h * half, half), :])
         y_start(3, h)
-    for step in near:
-        pl.semaphore_signal(met_sem, inc=1, device_id=ring_peer(step), device_id_type=MESH)
     copies[9].wait()
     copies[10].wait()
 
@@ -219,6 +219,9 @@
     def hops(k):
         return min(k // PLANE, runs - k // PLANE) + min(k % PLANE, PLANE - k % PLANE) // 2
 
+    for k in sorted(range(1, n_dp), key=hops, reverse=True):
+        d_send(k)
+    recv_d[held] = send_d[d]
     owner_half, _ = on_ring(z + mid)
     for p in range(2):
         ev_s[p] = v_ref[p, pl.ds(2 * y + owner_half, EX, stride=8), :]
@@ -226,10 +229,6 @@
         src_ref=ev_s, dst_ref=ev_r, send_sem=ev_sem.at[0], recv_sem=ev_sem.at[1], device_id=ring_peer(mid), device_id_type=MESH,
     )
     ev_copy.start()
-
-    for k in sorted(range(1, n_dp), key=hops, reverse=True):
-        d_send(k)
-    recv_d[held] = send_d[d]
     for i in range(YN):
         @pl.when(y != i)
         def _():

time: 37.1 us -> 36.6 us (0.987)
  Pallas kernels: 36.4 us -> 35.8 us
    pallas_call x1, Pallas kernels: 35.8 us -> 35.2 us  [shards(): pl.pallas_call(functools.partial(kernel, n_dp), out_shape=outs, in_specs=...]
where the time goes in v6:
time: 36.6 us; the launch traced here: 36.5 us
  Pallas kernels  35.8 us (98%)
  between operations  0.64 us (2%)
    pallas_call x1, Pallas kernels, shards(): pl.pallas_call(functools.partial(kernel, n_dp), out_shape=outs, in_specs=...  35.2 us

profile of v6, /device:TPU:1, one launch (start us, length us, event | category | flops | bytes accessed | tf_op | source)
XLA Modules:
  0.0 36.5 jit_solution(5212086494599354815)
XLA Ops:
  0.6 35.2 %shard_map.113 = (f32[2,4,128]{2,1,0:T(4,128)S(1)}, f32[1,32,128]{2,1,0:T(8,128)S(1)}) custom-call(bf16[256,1024]{1,0:T(8,128)(2,1)} %xo_ref.1, bf16[256,1024]{1,0:T(8,128)(2,1)} %go_ref.1, bf16[256,1024]{1,0:T(8,128)(2,1)} %xu_ref.1, bf16[256,3584]{1,0:T(8,128)(2,1)} %gu_ref.1, bf16[32,1024]{1,0:T(8,128)(2,1)} %bitcast.6, bf16[32,1024]{1,0:T(8,128)(2,1)} %bitcast.7, ...), custom_call_target="tpu_custom_call" | custom-call | tf_op jit(solution)/shard_map/pallas_call | solution.py:271
  35.8 0.6 %shard_map.114 = (f32[2,4,128]{2,1,0:T(4,128)}, f32[1,32,128]{2,1,0:T(8,128)}) custom-call(f32[2,4,128]{2,1,0:T(4,128)S(1)} %get-tuple-element.4.ev_ref, f32[1,32,128]{2,1,0:T(8,128)S(1)} %get-tuple-element.5.f_ref), custom_call_target="tpu_custom_call" | custom-call | tf_op jit(solution)/shard_map/pallas_call | solution.py:287

commit v7 on v6

--- a/solution.py
+++ b/solution.py
@@ -120,6 +120,9 @@
     copies[9].wait()
     copies[10].wait()
 
+    seg_copy = pltpu.make_async_remote_copy(
+        src_ref=seg_v, dst_ref=seg_r, send_sem=seg_sem.at[0], recv_sem=seg_sem.at[1], device_id=ring_peer(mid), device_id_type=MESH,
+    )
     swaps = []
     for h in range(2):
         total = part[y, h]
@@ -136,18 +139,16 @@
         swaps.append([
             pltpu.make_async_remote_copy(
                 src_ref=sum_z.at[h], dst_ref=recv_z.at[i, h], send_sem=sz_sem.at[i, h], recv_sem=rz_sem.at[i, h],
-                device_id=ring_peer(step), device_id_type=MESH,
+                device_id=ring_peer(mid * (1 - 2 * i)), device_id_type=MESH,
             )
-            for i, step in enumerate((mid, -mid))
+            for i in (core, 1 - core)
         ])
         for c in swaps[h]:
             c.start()
+        if h == 0:
+            seg_copy.start()
     for step in near[:2]:
         pl.semaphore_signal(known_sem, inc=1, device_id=ring_peer(step), device_id_type=MESH)
-    seg_copy = pltpu.make_async_remote_copy(
-        src_ref=seg_v, dst_ref=seg_r, send_sem=seg_sem.at[0], recv_sem=seg_sem.at[1], device_id=ring_peer(mid), device_id_type=MESH,
-    )
-    seg_copy.start()
     gathers = []
     for h in range(2):
         for c in swaps[h]:

time: 36.6 us -> 36.6 us (level)
  no operation moved by 1% of the time
where the time goes in v7:
time: 36.6 us; the launch traced here: 36.5 us
  Pallas kernels  35.8 us (98%)
  between operations  0.64 us (2%)
    pallas_call x1, Pallas kernels, shards(): pl.pallas_call(functools.partial(kernel, n_dp), out_shape=outs, in_specs=...  35.2 us

profile of v7, /device:TPU:1, one launch (start us, length us, event | category | flops | bytes accessed | tf_op | source)
XLA Modules:
  0.0 36.5 jit_solution(3661478188999137709)
XLA Ops:
  0.6 35.2 %shard_map.113 = (f32[2,4,128]{2,1,0:T(4,128)S(1)}, f32[1,32,128]{2,1,0:T(8,128)S(1)}) custom-call(bf16[256,1024]{1,0:T(8,128)(2,1)} %xo_ref.1, bf16[256,1024]{1,0:T(8,128)(2,1)} %go_ref.1, bf16[256,1024]{1,0:T(8,128)(2,1)} %xu_ref.1, bf16[256,3584]{1,0:T(8,128)(2,1)} %gu_ref.1, bf16[32,1024]{1,0:T(8,128)(2,1)} %bitcast.6, bf16[32,1024]{1,0:T(8,128)(2,1)} %bitcast.7, ...), custom_call_target="tpu_custom_call" | custom-call | tf_op jit(solution)/shard_map/pallas_call | solution.py:272
  35.8 0.6 %shard_map.114 = (f32[2,4,128]{2,1,0:T(4,128)}, f32[1,32,128]{2,1,0:T(8,128)}) custom-call(f32[2,4,128]{2,1,0:T(4,128)S(1)} %get-tuple-element.4.ev_ref, f32[1,32,128]{2,1,0:T(8,128)S(1)} %get-tuple-element.5.f_ref), custom_call_target="tpu_custom_call" | custom-call | tf_op jit(solution)/shard_map/pallas_call | solution.py:288
